TPU v7x, 256 devices: a whole 4x4x8 slice. The times are simulated.
256 devices in a mesh: mp: 16 (over y, x_hi, core), shard: 16 (over z, x_lo).
Axes of the slice: x: 4 (x_hi: 2, x_lo: 2; x = x_hi * 2 + x_lo), y: 4, z: 8, core: 2. Of those that a mesh axis runs over, the one named last changes fastest.
Arguments:
- bank: bfloat16 [4096, 8192], P('shard'), may hold values from -6 to 6
- calib_ids: int32 [16, 1024], P('mp', 'shard'), may hold values from 0 to 4095, as said below
- norm_gains: float32 [16, 8192], P('mp'), may hold values from 0.5 to 1.5
- proj_slabs: bfloat16 [16, 8192, 512], P('mp', 'shard'), may hold values from -0.0625 to 0.0625
Outputs:
- merged_gram: float32 [8192, 8192], P('mp', 'shard')
- numer: float32 [8192, 512], P('shard')
Inputs may be any that keep to these rules, and one draw needn't show every extreme that they name: `calib_ids`: token t of every model names a bank row in block t // 64, rows (t // 64) * 256 to (t // 64) * 256 + 255.
All inputs are finite; a program needn't handle non-finite values.
Results may differ from a plain program's by a relative error of at most 0.0048.
Values may be sent and summed in bfloat16 or wider, within the bound.
No kernel may reach another device: no remote copies, remote signals or barrier semaphores. Data moves between devices by JAX's collectives and lax.ppermute only.
A program may use at most 128 MiB of HBM per device.

v0:
```python
import jax
import jax.numpy as jnp
from jax import lax
from jax.sharding import PartitionSpec as P

ALPHA = 0.9
EPSILON = 1e-05


def local(bank, calib_ids, norm_gains, proj_slabs):
    model_width = bank.shape[1]
    bank_dev = bank.shape[0]
    col_block = model_width // lax.axis_size("shard")
    position = lax.axis_index("shard")
    local_ids = calib_ids[0] - position * bank_dev
    picked = jnp.take(bank, local_ids, axis=0).astype(jnp.float32)
    mean_square = jnp.mean(picked * picked, axis=-1, keepdims=True)
    calib_local = (picked * lax.rsqrt(mean_square + EPSILON) * norm_gains[0][None, :]).astype(
        jnp.bfloat16
    )
    calib = lax.all_gather(calib_local, "shard", axis=0, tiled=True)
    tokens = calib.shape[0]
    own_cols = lax.dynamic_slice_in_dim(calib, position * col_block, col_block, 1)
    own_float = own_cols.astype(jnp.float32)
    diag_part = jnp.sum(own_float * own_float, axis=0) / tokens
    weight_rows = proj_slabs[0]
    partial_out = jnp.dot(own_cols, weight_rows, preferred_element_type=jnp.float32)
    model_out = lax.psum(partial_out, "shard").astype(jnp.bfloat16)
    weighted = lax.dot_general(
        own_cols, model_out, (((0,), (0,)), ((), ())), preferred_element_type=jnp.float32
    )
    numer_part = ALPHA * weighted / tokens + (1.0 - ALPHA) * diag_part[
        :, None
    ] * weight_rows.astype(jnp.float32)
    product = lax.dot_general(
        calib, own_cols, (((0,), (0,)), ((), ())), preferred_element_type=jnp.float32
    )
    product = ALPHA * product / tokens
    row_index = lax.broadcasted_iota(jnp.int32, (model_width, col_block), 0)
    col_index = position * col_block + lax.broadcasted_iota(jnp.int32, (model_width, col_block), 1)
    merged_gram = lax.psum_scatter(
        product + jnp.where(row_index == col_index, (1.0 - ALPHA) * diag_part[None, :], 0.0),
        "mp",
        scatter_dimension=0,
        tiled=True,
    )
    numer = lax.psum(numer_part, "mp")
    return (merged_gram, numer)


def solution(mesh):
    placed = (P("shard", None), P("mp", "shard"), P("mp", None), P("mp", "shard", None))
    return jax.shard_map(
        local,
        mesh=mesh,
        in_specs=placed,
        out_specs=(P("mp", "shard"), P("shard", None)),
        check_vma=False,
    )
```

profile of v0, /device:TPU:1, one launch (start us, length us, event | category | flops | bytes accessed | tf_op | source)
XLA Modules:
  0.0 796.7 jit_solution(8639390773371479828)
XLA Ops:
  7.2 0.0 all-gather.2.cloned.1.call-start
  7.2 0.7 fusion.10
  7.9 0.7 compare_and_fusion
  8.5 4.9 gather_fusion
  13.4 0.5 fusion
  13.9 2.1 fusion.2
  16.0 0.0 all-gather.2.cloned.1.call-update
  16.0 0.0 all-reduce.3.cloned.1.call-start
  16.1 354.9 %all-gather.2.cloned.1.call-done = bf16[1024,8192]{1,0:T(8,128)(2,1)} async-done(((bf16[64,8192]{1,0:T(8,128)(2,1)}), bf16[1024,8192]{1,0:T(8,128)(2,1)}) %all-gather.2.cloned.1.call-update) | async-done | bytes 16777232 | tf_op jit(solution)/shard_map/all_gather | solution.py:21
  371.0 1.5 multiply_reduce_fusion
  372.5 2.1 fusion.6
  374.5 94.7 %all-reduce.4 = bf16[1024,512]{1,0:T(8,128)(2,1)S(1)} all-reduce(f32[1024,512]{1,0:T(8,128)S(1)} %fusion.6), channel_id=1, replica_groups=mesh['mp'=16,'shard'=16] {'shard'}, use_global_device_ids=true, to_apply=%region_3.4 | all-reduce | flops 524288 | bytes 3145728 | tf_op jit(solution)/shard_map/psum | solution.py:28
  469.3 3.1 fusion.3
  472.4 0.0 all-reduce.3.cloned.1.call-update
  472.4 0.0 reduce-scatter.2.cloned.1.call-start
  472.4 17.9 %select_add_fusion = f32[8192,512]{1,0:T(8,128)} fusion(bf16[1024,8192]{1,0:T(8,128)(2,1)} %all-gather.2.cloned.1.call-done, f32[512]{0:T(512)S(1)} %broadcast_multiply_fusion, s32[512]{0:T(512)S(1)} %iota_add_fusion, s32[]{:T(128)S(6)} %select_n.30), kind=kOutput, calls=%fused_computation.1 | convolution fusion | flops 8606711808 | bytes 34607108 | tf_op jit(solution)/shard_map/dot_general | solution.py:35
  490.3 0.0 reduce-scatter.2.cloned.1.call-update
  490.4 135.9 %all-reduce.3.cloned.1.call-done = f32[512,512]{1,0:T(8,128)} async-done(((f32[512,512]{1,0:T(8,128)}), f32[512,512]{1,0:T(8,128)}) %all-reduce.3.cloned.1.call-update) | async-done | bytes 1048592 | tf_op jit(solution)/shard_map/psum | solution.py:47
  626.2 161.7 %reduce-scatter.2.cloned.1.call-done = f32[512,512]{1,0:T(8,128)} async-done(((f32[8192,512]{1,0:T(8,128)}), f32[512,512]{1,0:T(8,128)}) %reduce-scatter.2.cloned.1.call-update) | async-done | bytes 1048592 | tf_op jit(solution)/shard_map/reduce_scatter | solution.py:41
  787.9 2.3 copy.9
  (4 shorter events, 0.0 us)
Async XLA Ops:
  7.2 363.8 %all-gather.2.cloned.1.call-start = ((), (), s32[]{:S(2)}) async-start(), calls=%async_computation.1 | async-start | bytes 17825792 | tf_op jit(solution)/shard_map/all_gather | solution.py:21
  16.0 610.2 %all-reduce.3.cloned.1.call-start = ((), (), s32[]{:S(2)}) async-start(), calls=%async_computation.3 | async-start | bytes 2097152 | tf_op jit(solution)/shard_map/psum | solution.py:47
  472.4 315.6 %reduce-scatter.2.cloned.1.call-start = ((), (), s32[]{:S(2)}) async-start(), calls=%async_computation.2 | async-start | bytes 17825792 | tf_op jit(solution)/shard_map/reduce_scatter | solution.py:41
Sparse Core Ops, SparseCore 0:
  16.2 354.7 all-gather.1
  472.5 153.6 all-reduce.2
  632.1 155.7 reduce-scatter.1
where the time goes:
time: 797 us
  waiting for transfers between devices  652 us (82%)
  blocking collectives  94.7 us (12%)
  matrix products  23 us (3%)
  between operations  13.8 us (2%)
    all_gather x1, waiting for transfers between devices, local(): calib = lax.all_gather(calib_local, 'shard', axis=0, tiled=True)  355 us
    reduce_scatter x1, waiting for transfers between devices, local(): lax.psum_scatter(product + jnp.where(row_index == col_index, (1.0 - ALPHA...  162 us
    psum x1, waiting for transfers between devices, local(): numer = lax.psum(numer_part, 'mp')  136 us
    psum x1, blocking collectives, local(): model_out = lax.psum(partial_out, 'shard').astype(jnp.bfloat16)  94.7 us
    dot_general x1, matrix products, local(): lax.dot_general(calib, own_cols, (((0,), (0,)), ((), ())), preferred_elem...  17.9 us
  transfers between devices with their start and end apart: 3, of which 3 were waited for; matrix products, arithmetic and copies ran while one was open for 2% of the time, Pallas kernels for 0%

commit v1 on v0

--- a/solution.py
+++ b/solution.py
@@ -5,6 +5,11 @@
 
 ALPHA = 0.9
 EPSILON = 1e-05
+
+
+def add_all(x, mesh_axis):
+    parts = lax.all_gather(x, mesh_axis)
+    return jnp.sum(parts, axis=0)
 
 
 def local(bank, calib_ids, norm_gains, proj_slabs):
@@ -44,7 +49,7 @@
         scatter_dimension=0,
         tiled=True,
     )
-    numer = lax.psum(numer_part, "mp")
+    numer = add_all(numer_part, "mp")
     return (merged_gram, numer)
 
 

time: 797 us -> 760 us (0.954)
  waiting for transfers between devices: 652 us -> 608 us
  other arithmetic: 5.41 us -> 14.3 us
    psum x1 -> x0, waiting for transfers between devices: 136 us -> none  [local(): numer = lax.psum(numer_part, 'mp')]
    all_gather x0 -> x1, waiting for transfers between devices: none -> 106 us  [add_all(): parts = lax.all_gather(x, mesh_axis)]
    reduce_scatter x1, waiting for transfers between devices: 162 us -> 148 us  [local(): lax.psum_scatter(product + jnp.where(row_index == col_index, (1.0 - ALPHA...]
    reduce_sum x0 -> x1, other arithmetic: none -> 8.88 us  [add_all(): return jnp.sum(parts, axis=0)]
  transfers between devices with their start and end apart: 3 -> 3, of which waited for: 3 -> 3; matrix products, arithmetic and copies ran while one was open for 2% -> 4% of each run, Pallas kernels for 0% -> 0%
where the time goes in v1:
time: 760 us; the launch traced here: 759 us
  waiting for transfers between devices  608 us (80%)
  blocking collectives  94.5 us (12%)
  matrix products  23 us (3%)
  other arithmetic  14.3 us (2%)
  between operations  13.8 us (2%)
    all_gather x1, waiting for transfers between devices, local(): calib = lax.all_gather(calib_local, 'shard', axis=0, tiled=True)  355 us
    reduce_scatter x1, waiting for transfers between devices, local(): lax.psum_scatter(product + jnp.where(row_index == col_index, (1.0 - ALPHA...  148 us
    all_gather x1, waiting for transfers between devices, add_all(): parts = lax.all_gather(x, mesh_axis)  106 us
    psum x1, blocking collectives, local(): model_out = lax.psum(partial_out, 'shard').astype(jnp.bfloat16)  94.5 us
    dot_general x1, matrix products, local(): lax.dot_general(calib, own_cols, (((0,), (0,)), ((), ())), preferred_elem...  17.9 us
  transfers between devices with their start and end apart: 3, of which 3 were waited for; matrix products, arithmetic and copies ran while one was open for 4% of the time, Pallas kernels for 0%

profile of v1, /device:TPU:1, one launch (start us, length us, event | category | flops | bytes accessed | tf_op | source)
XLA Modules:
  0.0 759.2 jit_solution(2730780854549361860)
XLA Ops:
  7.2 0.0 all-gather.4.cloned.1.call-start
  7.2 0.7 fusion.10
  7.9 0.7 compare_and_fusion
  8.5 4.9 gather_fusion
  13.4 0.5 fusion
  13.9 2.1 fusion.2
  16.0 0.0 all-gather.4.cloned.1.call-update
  16.0 0.0 all-gather.6.cloned.1.call-start
  16.1 354.9 %all-gather.4.cloned.1.call-done = bf16[1024,8192]{1,0:T(8,128)(2,1)} async-done(((bf16[64,8192]{1,0:T(8,128)(2,1)}), bf16[1024,8192]{1,0:T(8,128)(2,1)}) %all-gather.4.cloned.1.call-update) | async-done | bytes 16777232 | tf_op jit(solution)/shard_map/all_gather | solution.py:26
  371.0 1.5 multiply_reduce_fusion
  372.5 2.1 fusion.6
  374.5 94.5 %all-reduce.1 = bf16[1024,512]{1,0:T(8,128)(2,1)S(1)} all-reduce(f32[1024,512]{1,0:T(8,128)S(1)} %fusion.6), channel_id=1, replica_groups=mesh['mp'=16,'shard'=16] {'shard'}, use_global_device_ids=true, to_apply=%region_3.4 | all-reduce | flops 524288 | bytes 3145728 | tf_op jit(solution)/shard_map/psum | solution.py:33
  469.1 3.1 fusion.3
  472.2 0.0 all-gather.6.cloned.1.call-update
  472.2 0.2 reduce-scatter.2.cloned.1.call-start
  472.4 17.9 %select_add_fusion = f32[8192,512]{1,0:T(8,128)} fusion(bf16[1024,8192]{1,0:T(8,128)(2,1)} %all-gather.4.cloned.1.call-done, f32[512]{0:T(512)S(1)} %broadcast_multiply_fusion, s32[512]{0:T(512)S(1)} %iota_add_fusion, s32[]{:T(128)S(6)} %select_n.30), kind=kOutput, calls=%fused_computation.1 | convolution fusion | flops 8606711808 | bytes 34607108 | tf_op jit(solution)/shard_map/dot_general | solution.py:40
  490.3 0.0 reduce-scatter.2.cloned.1.call-update
  490.3 105.5 %all-gather.6.cloned.1.call-done = f32[8192,512]{1,0:T(8,128)} async-done(((f32[512,512]{1,0:T(8,128)}), f32[8192,512]{1,0:T(8,128)}) %all-gather.6.cloned.1.call-update) | async-done | bytes 16777232 | tf_op jit(solution)/shard_map/all_gather | solution.py:11
  595.8 8.9 %reduce_sum.29 = f32[512,512]{1,0:T(8,128)} reduce(f32[16,512,512]{2,1,0:T(8,128)} %bitcast.14, f32[]{:T(128)} %constant.20.clone.1), dimensions={0}, to_apply=%region_4.5 | reduce | flops 3932160 | bytes 17825796 | tf_op jit(solution)/shard_map/reduce_sum | solution.py:12
  604.7 148.0 %reduce-scatter.2.cloned.1.call-done = f32[512,512]{1,0:T(8,128)} async-done(((f32[8192,512]{1,0:T(8,128)}), f32[512,512]{1,0:T(8,128)}) %reduce-scatter.2.cloned.1.call-update) | async-done | bytes 1048592 | tf_op jit(solution)/shard_map/reduce_scatter | solution.py:46
  (4 shorter events, 0.0 us)
Async XLA Ops:
  7.2 363.8 %all-gather.4.cloned.1.call-start = ((), (), s32[]{:S(2)}) async-start(), calls=%async_computation.1 | async-start | bytes 17825792 | tf_op jit(solution)/shard_map/all_gather | solution.py:26
  16.0 579.8 %all-gather.6.cloned.1.call-start = ((), (), s32[]{:S(2)}) async-start(), calls=%async_computation.3 | async-start | bytes 17825792 | tf_op jit(solution)/shard_map/all_gather | solution.py:11
  472.2 280.5 %reduce-scatter.2.cloned.1.call-start = ((), (), s32[]{:S(2)}) async-start(), calls=%async_computation.2 | async-start | bytes 17825792 | tf_op jit(solution)/shard_map/reduce_scatter | solution.py:46
Sparse Core Ops, SparseCore 0:
  16.2 354.7 all-gather.3
  472.3 123.4 all-gather.5
  601.0 151.6 reduce-scatter.1
